TPU v7x, 32 devices: a whole 2x2x4 slice. The times are simulated.
32 devices in a mesh: blk: 16 (over z, y, x), slab: 2 (over core).
Axes of the slice: x: 2, y: 2, z: 4, core: 2. Of those that a mesh axis runs over, the one named last changes fastest.
Arguments:
- sinogram: bfloat16 [32, 8, 2048], P('blk', 'slab'), parts along dimension 1, may hold values from -6 to 6
- jitter: bfloat16 [32], P('blk'), may hold values from -0.29882812 to 0.29882812
- shift: int32 [32], replicated, may hold values from -8 to 8
Outputs:
- image: float32 [32, 8, 2048], P('blk', 'slab'), parts along dimension 1
There are 2 independent parts, one for each index of `slab`. A program takes and returns all parts, laid end to end along the dimension named above; an argument that names none is the same for every part. Nothing has to cross between parts.
All inputs are finite; a program needn't handle non-finite values.
Results may differ from a plain program's by a relative error of at most 0.0055.
Values may be sent and summed in bfloat16 or wider, within the bound.
A program may use at most 64 MiB of HBM per device.

v0:
```python
import math

import jax
import jax.numpy as jnp
from jax import lax
from jax.sharding import PartitionSpec as P

ROWS_DEV = 2


def padded(cells, sides, width):
    for axis, dim in sides:
        count = lax.axis_size(axis)
        head = lax.slice_in_dim(cells, 0, width, axis=dim)
        tail = lax.slice_in_dim(cells, cells.shape[dim] - width, cells.shape[dim], axis=dim)
        cells = jnp.concatenate(
            [
                lax.ppermute(tail, axis, [(i, (i + 1) % count) for i in range(count)]),
                cells,
                lax.ppermute(head, axis, [((i + 1) % count, i) for i in range(count)]),
            ],
            axis=dim,
        )
    return cells


def ramp_matrix(bins):
    offsets = (
        jnp.arange(bins, dtype=jnp.int32)[None, :] - jnp.arange(bins, dtype=jnp.int32)[:, None]
    )
    safe = jnp.where(offsets == 0, 1, offsets).astype(jnp.float32)
    odd_part = jnp.where(offsets % 2 != 0, -1.0 / (math.pi**2 * safe * safe), jnp.float32(0.0))
    kernel = jnp.where(offsets == 0, jnp.float32(0.25), odd_part)
    return kernel.astype(jnp.bfloat16)


def contribute(frow, theta, offset, row_count, nrows):
    slices, bins = frow.shape
    nblocks = bins // 128
    pad_tiles = bins // 512 + 2
    tile_count = nblocks + 2 * pad_tiles
    pad_bins = pad_tiles * 128
    tiled = jnp.pad(frow, ((0, 0), (pad_bins, pad_bins))).reshape(slices, tile_count, 128)
    coords_x = (jnp.arange(bins, dtype=jnp.float32) - (bins - 1) / 2).reshape(nblocks, 128)
    row_pos = jnp.arange(row_count, dtype=jnp.int32).astype(jnp.float32) - (nrows - 1) / 2
    cosine = jnp.cos(theta)
    sine_part = jnp.sin(theta)
    center_bin = (bins - 1) / 2 + offset.astype(jnp.float32)
    coords = coords_x[None, :, :] * cosine + row_pos[:, None, None] * sine_part + center_bin
    lowest = jnp.minimum(coords[:, :, 0], coords[:, :, 127])
    first_tile = jnp.clip(
        (jnp.floor(lowest).astype(jnp.int32) + pad_bins) // 128, 0, tile_count - 3
    )
    first_tile = first_tile.reshape(row_count * nblocks)
    wanted = first_tile[:, None] + jnp.arange(3, dtype=jnp.int32)[None, :]
    selector = (
        wanted[:, :, None] == jnp.arange(tile_count, dtype=jnp.int32)[None, None, :]
    ).astype(jnp.bfloat16)
    strips = jnp.einsum(
        "njt,stk->nsjk", selector, tiled, preferred_element_type=jnp.float32
    ).astype(jnp.bfloat16)
    strips = strips.reshape(row_count * nblocks, slices, 3 * 128)
    detector = (
        first_tile[:, None] * 128 + jnp.arange(3 * 128, dtype=jnp.int32)[None, :] - pad_bins
    ).astype(jnp.float32)
    flat_coords = coords.reshape(row_count * nblocks, 128)
    weights = jnp.maximum(
        0.0, 1.0 - jnp.abs(detector[:, :, None] - flat_coords[:, None, :])
    ).astype(jnp.bfloat16)
    return jnp.einsum("nsb,nbc->nsc", strips, weights, preferred_element_type=jnp.float32)


def body(sinogram, jitter, shift):
    ang_dev, slices, bins = sinogram.shape
    width = lax.axis_size("blk")
    angles = width * ang_dev
    nrows = ROWS_DEV * width
    nblocks = bins // 128
    here = lax.axis_index("blk")
    extended = padded(jitter, (("blk", 0),), 1).astype(jnp.float32)
    weight = (1.0 + (extended[2:] - extended[:-2]) * 1.5) * (4.0 / math.sqrt(angles))
    ramp = ramp_matrix(bins)
    flat = jnp.dot(
        sinogram.reshape(ang_dev * slices, bins), ramp, preferred_element_type=jnp.float32
    )
    filtered = (flat.reshape(ang_dev, slices, bins) * weight[:, None, None]).astype(jnp.bfloat16)
    first = here * ang_dev
    count = ROWS_DEV * lax.axis_size("blk")

    def one_angle(position, accum):
        angle_id = first + position
        deviation = lax.dynamic_index_in_dim(jitter, position, 0, False).astype(jnp.float32)
        theta = (angle_id.astype(jnp.float32) + deviation) * math.pi / angles
        offset = lax.dynamic_index_in_dim(shift, angle_id, 0, False)
        frow = lax.dynamic_index_in_dim(filtered, position, 0, False)
        return accum + contribute(frow, theta, offset, count, nrows)

    accum = lax.fori_loop(
        0, ang_dev, one_angle, jnp.zeros((count * nblocks, slices, 128), jnp.float32)
    )
    return lax.psum_scatter(
        accum.reshape(count, nblocks, slices, 128)
        .transpose(0, 2, 1, 3)
        .reshape(count, slices, bins),
        "blk",
        scatter_dimension=0,
        tiled=True,
    )


def solution(mesh):
    in_specs = (P("blk", "slab", None), P("blk"), P())
    out_specs = P("blk", "slab", None)
    return jax.shard_map(body, mesh=mesh, in_specs=in_specs, out_specs=out_specs, check_vma=False)
```

profile of v0, /device:TPU:0, one launch (start us, length us, event | category | flops | bytes accessed | tf_op | source)
XLA Modules:
  0.0 243.2 jit_solution(2400293270538522140)
XLA Ops:
  6.5 1.3 fusion.38
  7.9 3.0 %collective-permute-start = (bf16[1]{0:T(256)(128)(2,1)}, bf16[1]{0:T(256)(128)(2,1)}, u32[]{:S(2)}, u32[]{:S(2)}) collective-permute-start(bf16[1]{0:T(256)(128)(2,1)} %get-tuple-element.201), channel_id=1, source_target_pairs={{0,2},{2,4},{4,6},{6,8},{8,10},{10,12},{12,14},{14,16},{16,18},{18... | collective-permute-start | bytes 14 | tf_op jit(solution)/shard_map/ppermute | solution.py:18
  10.8 4.0 %collective-permute-start.1 = (bf16[1]{0:T(256)(128)(2,1)}, bf16[1]{0:T(256)(128)(2,1)}, u32[]{:S(2)}, u32[]{:S(2)}) collective-permute-start(bf16[1]{0:T(256)(128)(2,1)} %get-tuple-element.202), channel_id=1, source_target_pairs={{2,0},{4,2},{6,4},{8,6},{10,8},{12,10},{14,12},{16,14},{18,16},{20... | collective-permute-start | bytes 14 | tf_op jit(solution)/shard_map/ppermute | solution.py:20
  14.8 0.8 reshape.204
  15.6 13.4 %fusion.27 = f32[8,2048]{1,0:T(8,128)S(1)} fusion(bf16[8,2048]{1,0:T(8,128)(2,1)S(1)} %reshape.204), kind=kOutput, calls=%fused_computation.49 | convolution fusion | flops 159383552 | bytes 98304 | tf_op jit(solution)/shard_map/dot_general | solution.py:83
  29.1 1.3 maximum_convert_fusion.4
  30.6 91.1 %while.16 = (s32[]{:T(128)}, f32[512,4,128]{2,1,0:T(4,128)}, bf16[2,4,2048]{2,1,0:T(4,128)(2,1)S(1)}, s32[]{:T(128)}, bf16[2]{0:T(256)(128)(2,1)S(1)}, /*index=5...) while((s32[]{:T(128)}, f32[512,4,128]{2,1,0:T(4,128)}, ...), condition=%wide.region_1.2_spmd.clone, body=%wide.region_0.1_spmd.clone.sunk | while | flops 373422176 | bytes 10977945 | solution.py:98
  30.6 0.6 dynamic_slice.41
  31.9 0.7 dynamic_slice.42
  33.5 0.7 fusion.51
  34.4 0.6 convolution_convert_fusion.2
  35.0 1.4 copy.17
  36.9 39.0 %fusion.53 = f32[512,4,128]{2,1,0:T(4,128)} fusion(bf16[512,4,384]{2,1,0:T(4,128)(2,1)S(1)} %copy.17, f32[512,128]{1,0:T(8,128)S(1)} %fusion.52, f32[512,384]{1,0:T(8,128)S(1)} %add_convert_fusion.2, f32[512,4,128]{2,1,0:T(4,128)} %get-tuple-element.257, pred[]{:T(512)S(6)} %compare.34), kind=kOutput, calls=%fused_computation.3.clone.2 | convolution fusion | flops 327680000 | bytes 4718593 | tf_op jit(solution)/shard_map/while/body/eval_jaxpr/nsb,nbc->nsc/dot_general | solution.py:70
  75.9 0.6 dynamic_slice.41
  77.1 0.7 dynamic_slice.42
  78.7 0.7 fusion.51
  79.6 0.6 convolution_convert_fusion.2
  80.2 1.4 copy.17
  82.1 39.6 %fusion.53 = f32[512,4,128]{2,1,0:T(4,128)} fusion(bf16[512,4,384]{2,1,0:T(4,128)(2,1)S(1)} %copy.17, f32[512,128]{1,0:T(8,128)S(1)} %fusion.52, f32[512,384]{1,0:T(8,128)S(1)} %add_convert_fusion.2, f32[512,4,128]{2,1,0:T(4,128)} %get-tuple-element.257, pred[]{:T(512)S(6)} %compare.34), kind=kOutput, calls=%fused_computation.3.clone.2 | convolution fusion | flops 327680000 | bytes 4718593 | tf_op jit(solution)/shard_map/while/body/eval_jaxpr/nsb,nbc->nsc/dot_general | solution.py:70
  121.7 1.3 copy.15
  123.1 1.4 reshape.207
  124.5 0.6 dynamic-slice
  125.7 109.2 %all-reduce.4.cloned.1.call-done = f32[32,4,2048]{2,1,0:T(4,128)} async-done(((f32[32,4,2048]{2,1,0:T(4,128)}), f32[32,4,2048]{2,1,0:T(4,128)}) %all-reduce.4.cloned.1.call-update) | async-done | bytes 1048592
  234.8 1.5 constant_dynamic-slice_fusion
  (40 shorter events, 1.7 us)
Async XLA Ops:
  6.5 228.3 %all-reduce.4.cloned.1.call-start = ((), (), s32[]{:S(2)}) async-start(), calls=%async_computation | async-start | bytes 2097152
  7.9 21.2 %collective-permute-start = (bf16[1]{0:T(256)(128)(2,1)}, bf16[1]{0:T(256)(128)(2,1)}, u32[]{:S(2)}, u32[]{:S(2)}) collective-permute-start(bf16[1]{0:T(256)(128)(2,1)} %get-tuple-element.201), channel_id=1, source_target_pairs={{0,2},{2,4},{4,6},{6,8},{8,10},{10,12},{12,14},{14,16},{16,18},{18... | collective-permute-start | bytes 14 | tf_op jit(solution)/shard_map/ppermute | solution.py:18
  10.8 18.3 %collective-permute-start.1 = (bf16[1]{0:T(256)(128)(2,1)}, bf16[1]{0:T(256)(128)(2,1)}, u32[]{:S(2)}, u32[]{:S(2)}) collective-permute-start(bf16[1]{0:T(256)(128)(2,1)} %get-tuple-element.202), channel_id=1, source_target_pairs={{2,0},{4,2},{6,4},{8,6},{10,8},{12,10},{14,12},{16,14},{18,16},{20... | collective-permute-start | bytes 14 | tf_op jit(solution)/shard_map/ppermute | solution.py:20
  15.6 13.5 %copy-start = (bf16[2]{0:T(256)(128)(2,1)S(1)}, bf16[2]{0:T(256)(128)(2,1)}, u32[]{:S(2)}) copy-start(bf16[2]{0:T(256)(128)(2,1)} %param.6) | copy-start | bytes 16
  15.6 15.0 %copy-start.1 = (s32[32]{0:T(128)S(1)}, s32[32]{0:T(128)}, u32[]{:S(2)}) copy-start(s32[32]{0:T(128)} %param.7) | copy-start | bytes 388
  123.0 1.4 copy-start.2
Sparse Core Ops, SparseCore 0:
  124.6 110.2 all-reduce.3
where the time goes:
time: 244 us; the launch traced here: 243 us
  waiting for transfers between devices  109 us (45%)
  matrix products  93.2 us (38%)
  between operations  14.1 us (6%)
  local copies, waits for them, and re-layouts  12.9 us (5%)
  starting transfers between devices  6.97 us (3%)
  other arithmetic  3.74 us (2%)
  loops' own time  3.06 us (1%)
    unnamed x2, waiting for transfers between devices  109 us
    dot_general x2, matrix products, contribute(): jnp.einsum('nsb,nbc->nsc', strips, weights, preferred_element_type=jnp.fl...  78.6 us
    dot_general x1, matrix products, body(): jnp.dot(sinogram.reshape(ang_dev * slices, bins), ramp, preferred_element...  13.4 us
  transfers between devices with their start and end apart: 3, of which 1 were waited for; matrix products, arithmetic and copies ran while one was open for 6% of the time, Pallas kernels for 0%

commit v1 on v0

v1 whole, which is shorter than its diff:
```python
import functools
import math

import jax
import jax.numpy as jnp
import numpy as np
from jax import lax
from jax.experimental import pallas as pl
from jax.experimental.pallas import tpu as pltpu
from jax.sharding import PartitionSpec as P

LANES = 128
SUBS = 8
BLOCK = 256
PLANE = 4
MESH = pl.DeviceIdType.MESH


def ramp_slab(bins):
    span = 2 * bins - BLOCK
    offsets = (
        np.arange(span, dtype=np.int32)[None, :]
        - np.int32(bins - BLOCK)
        - np.arange(BLOCK, dtype=np.int32)[:, None]
    )
    safe = np.where(offsets == 0, 1, offsets).astype(np.float32)
    odd_part = np.where(
        offsets % 2 != 0, np.float32(-1.0) / (np.float32(math.pi**2) * safe * safe), np.float32(0)
    )
    return np.where(offsets == 0, np.float32(0.25), odd_part).astype(jnp.bfloat16)


def kernel(
    width,
    jit_ref,
    shift_ref,
    sino_ref,
    slab_hbm,
    out_ref,
    slab,
    chunks,
    jmsg,
    jall,
    pvec,
    psm,
    fval,
    fdif,
    acc,
    lsem,
    sj,
    rj,
    sz,
    rz,
    sx,
    rx,
    sy,
    ry,
    sd,
    rd,
):
    me = lax.axis_index("blk")
    ang_dev, slices, bins = sino_ref.shape
    rows_dev = out_ref.shape[0]
    angles = width * ang_dev
    nrows = width * rows_dev
    nblocks = bins // LANES
    ntiles = fval.shape[1]
    depth = width // PLANE
    px, py = me % 2, (me // 2) % 2
    xpeer = me + 1 - 2 * px
    ypeer = me + 2 - 4 * py
    diag = me + 1 - 2 * px + 2 - 4 * py

    def remote(src, dst, send, recv, dev):
        return pltpu.make_async_remote_copy(
            src_ref=src,
            dst_ref=dst,
            send_sem=send,
            recv_sem=recv,
            device_id={"blk": dev},
            device_id_type=MESH,
        )

    def at(dev, k):
        return (dev + width - PLANE * k) % width

    def zcopy(k):
        return remote(
            chunks.at[me], chunks.at[me], sz.at[k], rz.at[k], (me + PLANE * k) % width
        )

    def xcopy(k):
        c = at(me, k)
        return remote(chunks.at[c], chunks.at[c], sx.at[k], rx.at[k], xpeer)

    def ycopy(k):
        c = at(me, k)
        return remote(chunks.at[c], chunks.at[c], sy.at[k], ry.at[k], ypeer)

    def relay_x(k):
        c = at(xpeer, k)
        return remote(
            chunks.at[c, 0], chunks.at[c, 0], sd.at[0, k], rd.at[0, k], ypeer
        )

    def relay_y(k):
        c = at(ypeer, k)
        return remote(
            chunks.at[c, 1], chunks.at[c, 1], sd.at[1, k], rd.at[1, k], xpeer
        )

    def jcopy(i):
        return remote(jmsg, jall.at[me], sj.at[i], rj.at[i], (me + i) % width)

    barrier = pltpu.get_barrier_semaphore()

    @pl.loop(1, width)
    def _(i):
        pl.semaphore_signal(
            barrier, inc=1, device_id={"blk": (me + i) % width}, device_id_type=MESH
        )

    load = pltpu.make_async_copy(slab_hbm, slab, lsem.at[0])
    load.start()

    lane = lax.broadcasted_iota(jnp.int32, (SUBS, LANES), 1)
    sub = lax.broadcasted_iota(jnp.int32, (SUBS, LANES), 0)
    lanef = lane.astype(jnp.float32)
    mine = (lane % angles) - me * ang_dev
    msg = jnp.zeros((SUBS, LANES), jnp.float32)
    for i in range(ang_dev):
        msg = jnp.where(mine == i, jit_ref[i], msg)
    jmsg[...] = msg
    jall[me] = msg
    zero = jnp.zeros((SUBS, LANES), jnp.float32)
    for i in range(ang_dev):
        for t in [0] + list(range(nblocks + 1, ntiles)):
            fval[i, t] = zero
            fdif[i, t] = zero
    for b in range(nblocks):
        acc[b] = zero

    nb = bins // BLOCK
    flat = jnp.concatenate(
        [sino_ref[i].astype(jnp.float32) for i in range(ang_dev)], axis=0
    )
    lhs = jnp.concatenate(
        [flat[:, i * BLOCK : (i + 1) * BLOCK] for i in range(nb)], axis=0
    ).astype(jnp.bfloat16)
    load.wait()
    total = [None] * nb
    for d in range(2 * nb - 1):
        prod = jnp.dot(
            lhs, slab[:, d * BLOCK : (d + 1) * BLOCK], preferred_element_type=jnp.float32
        )
        for i in range(nb):
            j = d - (nb - 1) + i
            if 0 <= j < nb:
                piece = prod[i * SUBS : (i + 1) * SUBS]
                total[j] = piece if total[j] is None else total[j] + piece
    row = jnp.concatenate(total, axis=1)
    quarter = bins // 4
    for h in range(2):
        chunks[me, h] = jnp.concatenate(
            [row[:, (2 * h + q) * quarter : (2 * h + q + 1) * quarter] for q in range(2)], axis=0
        ).astype(jnp.bfloat16)

    pl.semaphore_wait(barrier, width - 1)

    @pl.loop(1, width)
    def _(i):
        jcopy(i).start()

    @pl.loop(1, depth)
    def _(k):
        zcopy(k).start()

    xcopy(0).start()
    ycopy(0).start()

    @pl.loop(1, width)
    def _(i):
        jcopy(i).wait()

    jit = jall[0]
    for i in range(1, width):
        jit = jit + jall[i]
    ahead = pltpu.roll(jit, LANES - 1, 1)
    behind = pltpu.roll(jit, 1, 1)
    weight = (1.0 + (ahead - behind) * 1.5) * (4.0 / math.sqrt(angles))
    theta = ((lane % angles).astype(jnp.float32) + jit) * math.pi / angles
    pvec[...] = jnp.where(
        sub == 0, jnp.cos(theta), jnp.where(sub == 1, jnp.sin(theta), weight)
    )
    move = pltpu.make_async_copy(pvec, psm, lsem.at[1])
    move.start()
    move.wait()

    half = (bins - 1) / 2
    first_row = (me * rows_dev).astype(jnp.float32) - (nrows - 1) / 2
    rowf = (sub // slices).astype(jnp.float32) + first_row
    low_half = sub < slices

    def project(chunk):
        after = [None] * ang_dev
        wts = [psm[2, chunk * ang_dev + i] for i in range(ang_dev)]
        for t in range(nblocks - 1, -2, -1):
            if t >= 0:
                h, q, k = t // (nblocks // 2), (t // (nblocks // 4)) % 2, t % (nblocks // 4)
                tile = chunks[
                    chunk, h, q * SUBS : (q + 1) * SUBS, k * LANES : (k + 1) * LANES
                ].astype(jnp.float32)
                turned = pltpu.roll(tile, slices, 0)
                pair = [
                    jnp.where(low_half, tile, turned) * wts[0],
                    jnp.where(low_half, turned, tile) * wts[1],
                ]
            else:
                pair = [zero] * ang_dev
            for i in range(ang_dev):
                rolled = pltpu.roll(pair[i], LANES - 1, 1)
                nxt = zero if after[i] is None else after[i]
                fdif[i, t + 1] = jnp.where(lane == LANES - 1, nxt, rolled) - pair[i]
                if t >= 0:
                    fval[i, t + 1] = pair[i]
                after[i] = rolled
        for i in range(ang_dev):
            a = chunk * ang_dev + i
            cosine = psm[0, a]
            sine = psm[1, a]
            center = half + shift_ref[a].astype(jnp.float32)
            ramp = lanef * cosine + rowf * sine
            least = jnp.minimum(cosine * (LANES - 1), 0.0) + jnp.minimum(
                first_row * sine, (first_row + (rows_dev - 1)) * sine
            )
            for b in range(nblocks):
                base = (b * LANES - half) * cosine + center + LANES
                low = (base + least - 0.25).astype(jnp.int32) // LANES
                low = jnp.minimum(jnp.maximum(low, 0), ntiles - 2)
                u = ramp + (base - (low * LANES).astype(jnp.float32))
                bin_lo = u.astype(jnp.int32)
                frac = u - bin_lo.astype(jnp.float32)
                where = jnp.bitwise_and(bin_lo, LANES - 1)
                first = bin_lo < LANES

                def pick(ref):
                    return jnp.where(
                        first,
                        jnp.take_along_axis(ref[i, low], where, axis=1, mode="promise_in_bounds"),
                        jnp.take_along_axis(
                            ref[i, low + 1], where, axis=1, mode="promise_in_bounds"
                        ),
                    )

                acc[b] += pick(fval) + frac * pick(fdif)

    def relay(k):
        xcopy(k).wait_recv()
        relay_x(k).start()
        ycopy(k).wait_recv()
        relay_y(k).start()

    def corner(k):
        relay_x(k).wait_recv()
        relay_y(k).wait_recv()
        project(at(diag, k))

    project(me)
    relay(0)

    @pl.loop(1, depth)
    def _(k):
        zcopy(k).wait_recv()
        xcopy(k).start()
        ycopy(k).start()
        project(at(xpeer, k - 1))
        project(at(ypeer, k - 1))
        project(at(me, k))
        relay(k)
        corner(k - 1)

    project(at(xpeer, depth - 1))
    project(at(ypeer, depth - 1))
    corner(depth - 1)

    for b in range(nblocks):
        done = acc[b]
        for r in range(rows_dev):
            out_ref[r, :, b * LANES : (b + 1) * LANES] = done[r * slices : (r + 1) * slices]

    @pl.loop(0, depth)
    def _(k):
        xcopy(k).wait_send()
        ycopy(k).wait_send()
        relay_x(k).wait_send()
        relay_y(k).wait_send()

    @pl.loop(1, depth)
    def _(k):
        zcopy(k).wait_send()


def body(sinogram, jitter, shift):
    width = lax.axis_size("blk")
    ang_dev, slices, bins = sinogram.shape
    angles = shift.shape[0]
    rows_dev = SUBS // slices
    assert ang_dev == 2 and ang_dev * slices == SUBS and LANES % angles == 0
    assert width % PLANE == 0 and bins % (2 * BLOCK) == 0
    depth = width // PLANE
    ntiles = bins // LANES + 3
    vmem = pl.BlockSpec(memory_space=pltpu.VMEM)
    smem = pl.BlockSpec(memory_space=pltpu.SMEM)
    dma = pltpu.SemaphoreType.DMA
    slab = jnp.asarray(ramp_slab(bins))
    return pl.pallas_call(
        functools.partial(kernel, width),
        out_shape=jax.ShapeDtypeStruct((rows_dev, slices, bins), jnp.float32),
        in_specs=[smem, smem, vmem, pl.BlockSpec(memory_space=pl.ANY)],
        out_specs=vmem,
        scratch_shapes=[
            pltpu.VMEM(slab.shape, jnp.bfloat16),
            pltpu.VMEM((width, 2, 2 * SUBS, bins // 4), jnp.bfloat16),
            pltpu.VMEM((SUBS, LANES), jnp.float32),
            pltpu.VMEM((width, SUBS, LANES), jnp.float32),
            pltpu.VMEM((SUBS, LANES), jnp.float32),
            pltpu.SMEM((SUBS, LANES), jnp.float32),
            pltpu.VMEM((ang_dev, ntiles, SUBS, LANES), jnp.float32),
            pltpu.VMEM((ang_dev, ntiles, SUBS, LANES), jnp.float32),
            pltpu.VMEM((bins // LANES, SUBS, LANES), jnp.float32),
            dma((2,)),
            dma((width,)),
            dma((width,)),
            dma((depth,)),
            dma((depth,)),
            dma((depth,)),
            dma((depth,)),
            dma((depth,)),
            dma((depth,)),
            dma((2, depth)),
            dma((2, depth)),
        ],
        compiler_params=pltpu.CompilerParams(collective_id=0, has_side_effects=True),
    )(jitter.astype(jnp.float32), shift, sinogram, slab)


def solution(mesh):
    in_specs = (P("blk", "slab", None), P("blk"), P())
    out_specs = P("blk", "slab", None)
    return jax.shard_map(body, mesh=mesh, in_specs=in_specs, out_specs=out_specs, check_vma=False)
```

time: 244 us -> 30.4 us (0.12)
  waiting for transfers between devices: 109 us -> 0 us
  matrix products: 93.2 us -> 0 us
  Pallas kernels: 0 us -> 27.5 us
  between operations: 14.1 us -> 0.01 us
  local copies, waits for them, and re-layouts: 12.9 us -> 1.47 us
  starting transfers between devices: 6.97 us -> 0 us
  loops' own time: 3.06 us -> 0 us
  other arithmetic: 3.74 us -> 1.17 us
    unnamed x2 -> x0, waiting for transfers between devices: 109 us -> none
    dot_general x5 -> x0, matrix products: 93.2 us -> none  [the longest x2 78.6 us: contribute(): jnp.einsum('nsb,nbc->nsc', strips, weights, preferred_element_type=jnp.fl...]
    pallas_call x0 -> x1, Pallas kernels: none -> 27.5 us  [body(): pl.pallas_call(functools.partial(kernel, width), out_shape=jax.ShapeDtype...]
    ppermute x2 -> x0, starting transfers between devices: 6.96 us -> none  [the longest x1 4 us: padded(): lax.ppermute(head, axis, [((i + 1) % count, i) for i in range(count)])]
    reshape x8 -> x0, local copies, waits for them, and re-layouts: 6.45 us -> none  [the longest x2 2.89 us: contribute(): strips = strips.reshape(row_count * nblocks, slices, 3 * 128)]
    another operation x1 -> x0, loops' own time: 3.06 us -> none  [body(): lax.fori_loop(0, ang_dev, one_angle, jnp.zeros((count * nblocks, slices,...]
    dynamic_slice x4 -> x0, local copies, waits for them, and re-layouts: 2.52 us -> none  [the longest x2 1.3 us: one_angle(): lax.dynamic_index_in_dim(jitter, position, 0, False).astype(jnp.float32)]
  transfers between devices with their start and end apart: 3 -> 0, of which waited for: 1 -> 0; matrix products, arithmetic and copies ran while one was open for 6% -> 0% of each run, Pallas kernels for 0% -> 0%
where the time goes in v1:
time: 30.4 us; the launch traced here: 30.1 us
  Pallas kernels  27.5 us (90%)
  local copies, waits for them, and re-layouts  1.47 us (5%)
  other arithmetic  1.17 us (4%)
    pallas_call x1, Pallas kernels, body(): pl.pallas_call(functools.partial(kernel, width), out_shape=jax.ShapeDtype...  27.5 us
    unnamed x1, local copies, waits for them, and re-layouts  1.47 us
    convert_element_type x1, other arithmetic, body(): jitter.astype(jnp.float32)  1.17 us

profile of v1, /device:TPU:0, one launch (start us, length us, event | category | flops | bytes accessed | tf_op | source)
XLA Modules:
  0.0 30.1 jit_solution(12818257104872236595)
XLA Ops:
  0.0 1.2 %convert_element_type.3.jit_ref = f32[2]{0:T(128)} convert(bf16[2]{0:T(256)(128)(2,1)} %param.5) | non-fusion elementwise | flops 2 | bytes 12 | tf_op jit(solution)/shard_map/convert_element_type | solution.py:344
  1.2 27.5 %shard_map.46 = f32[2,4,2048]{2,1,0:T(4,128)} custom-call(f32[2]{0:T(128)} %convert_element_type.3.jit_ref, s32[32]{0:T(128)} %shift_ref.1, bf16[2,4,2048]{2,1,0:T(4,128)(2,1)} %sino_ref.1, bf16[256,3840]{1,0:T(8,128)(2,1)} %constant.2.clone.slab_hbm), custom_call_target="tpu_custom_call" | custom-call | tf_op jit(solution)/shard_map/pallas_call | solution.py:316
  28.7 1.5 %copy.6 = f32[2,4,2048]{2,1,0:T(4,128)} copy(f32[2,4,2048]{2,1,0:T(4,128)} %shard_map.46) | data formatting | bytes 131072

commit v2 on v1

--- a/solution.py
+++ b/solution.py
@@ -112,6 +112,12 @@
     def jcopy(i):
         return remote(jmsg, jall.at[me], sj.at[i], rj.at[i], (me + i) % width)
 
+    def relay(k):
+        xcopy(k).wait_recv()
+        relay_x(k).start()
+        ycopy(k).wait_recv()
+        relay_y(k).start()
+
     barrier = pltpu.get_barrier_semaphore()
 
     @pl.loop(1, width)
@@ -129,7 +135,7 @@
     mine = (lane % angles) - me * ang_dev
     msg = jnp.zeros((SUBS, LANES), jnp.float32)
     for i in range(ang_dev):
-        msg = jnp.where(mine == i, jit_ref[i], msg)
+        msg = jnp.where(mine == i, jit_ref[0:1, i : i + 1].astype(jnp.float32), msg)
     jmsg[...] = msg
     jall[me] = msg
     zero = jnp.zeros((SUBS, LANES), jnp.float32)
@@ -177,6 +183,14 @@
 
     xcopy(0).start()
     ycopy(0).start()
+
+    relay(0)
+
+    @pl.loop(1, depth)
+    def _(k):
+        zcopy(k).wait_recv()
+        xcopy(k).start()
+        ycopy(k).start()
 
     @pl.loop(1, width)
     def _(i):
@@ -254,34 +268,26 @@
 
                 acc[b] += pick(fval) + frac * pick(fdif)
 
-    def relay(k):
-        xcopy(k).wait_recv()
-        relay_x(k).start()
-        ycopy(k).wait_recv()
-        relay_y(k).start()
-
     def corner(k):
         relay_x(k).wait_recv()
         relay_y(k).wait_recv()
         project(at(diag, k))
 
     project(me)
-    relay(0)
 
     @pl.loop(1, depth)
     def _(k):
-        zcopy(k).wait_recv()
-        xcopy(k).start()
-        ycopy(k).start()
+        relay(k)
+        project(at(me, k))
         project(at(xpeer, k - 1))
         project(at(ypeer, k - 1))
-        project(at(me, k))
-        relay(k)
-        corner(k - 1)
 
     project(at(xpeer, depth - 1))
     project(at(ypeer, depth - 1))
-    corner(depth - 1)
+
+    @pl.loop(0, depth)
+    def _(k):
+        corner(k)
 
     for b in range(nblocks):
         done = acc[b]
@@ -315,8 +321,8 @@
     slab = jnp.asarray(ramp_slab(bins))
     return pl.pallas_call(
         functools.partial(kernel, width),
-        out_shape=jax.ShapeDtypeStruct((rows_dev, slices, bins), jnp.float32),
-        in_specs=[smem, smem, vmem, pl.BlockSpec(memory_space=pl.ANY)],
+        out_shape=pltpu.VMEM((rows_dev, slices, bins), jnp.float32),
+        in_specs=[vmem, smem, vmem, pl.BlockSpec(memory_space=pl.ANY)],
         out_specs=vmem,
         scratch_shapes=[
             pltpu.VMEM(slab.shape, jnp.bfloat16),
@@ -341,7 +347,7 @@
             dma((2, depth)),
         ],
         compiler_params=pltpu.CompilerParams(collective_id=0, has_side_effects=True),
-    )(jitter.astype(jnp.float32), shift, sinogram, slab)
+    )(jitter.reshape(1, ang_dev), shift, sinogram, slab)
 
 
 def solution(mesh):

time: 30.4 us -> 22.4 us (0.74)
  Pallas kernels: 27.5 us -> 21.6 us
  other arithmetic: 1.17 us -> 0 us
  local copies, waits for them, and re-layouts: 1.47 us -> 0.63 us
    pallas_call x1, Pallas kernels: 27.5 us -> 21.6 us  [body(): pl.pallas_call(functools.partial(kernel, width), out_shape=pltpu.VMEM((ro...]
    convert_element_type x1 -> x0, other arithmetic: 1.17 us -> none  [body(): jitter.astype(jnp.float32)]
    unnamed x1, local copies, waits for them, and re-layouts: 1.47 us -> 0.63 us
where the time goes in v2:
time: 22.4 us; the launch traced here: 22.2 us
  Pallas kernels  21.6 us (96%)
  local copies, waits for them, and re-layouts  0.63 us (3%)
    pallas_call x1, Pallas kernels, body(): pl.pallas_call(functools.partial(kernel, width), out_shape=pltpu.VMEM((ro...  21.6 us
    unnamed x1, local copies, waits for them, and re-layouts  0.63 us

profile of v2, /device:TPU:0, one launch (start us, length us, event | category | flops | bytes accessed | tf_op | source)
XLA Modules:
  0.0 22.2 jit_solution(5556068834200987969)
XLA Ops:
  0.0 21.6 %shard_map.46 = f32[2,4,2048]{2,1,0:T(4,128)S(1)} custom-call(bf16[1,2]{1,0:T(2,128)(2,1)} %bitcast.1, s32[32]{0:T(128)} %shift_ref.1, bf16[2,4,2048]{2,1,0:T(4,128)(2,1)} %sino_ref.1, bf16[256,3840]{1,0:T(8,128)(2,1)} %constant.2.clone.slab_hbm), custom_call_target="tpu_custom_call" | custom-call | tf_op jit(solution)/shard_map/pallas_call | solution.py:322
  21.6 0.6 %copy.6 = f32[2,4,2048]{2,1,0:T(4,128)} copy(f32[2,4,2048]{2,1,0:T(4,128)S(1)} %shard_map.46) | data formatting | bytes 131072

commit v3 on v2

--- a/solution.py
+++ b/solution.py
@@ -43,6 +43,8 @@
     jall,
     pvec,
     psm,
+    tvec,
+    tsm,
     fval,
     fdif,
     acc,
@@ -64,7 +66,7 @@
     angles = width * ang_dev
     nrows = width * rows_dev
     nblocks = bins // LANES
-    ntiles = fval.shape[1]
+    ntiles = fval.shape[2]
     depth = width // PLANE
     px, py = me % 2, (me // 2) % 2
     xpeer = me + 1 - 2 * px
@@ -132,17 +134,18 @@
     lane = lax.broadcasted_iota(jnp.int32, (SUBS, LANES), 1)
     sub = lax.broadcasted_iota(jnp.int32, (SUBS, LANES), 0)
     lanef = lane.astype(jnp.float32)
-    mine = (lane % angles) - me * ang_dev
-    msg = jnp.zeros((SUBS, LANES), jnp.float32)
+    mine = (lane[:1] % angles) - me * ang_dev
+    msg = jnp.zeros((1, LANES), jnp.float32)
     for i in range(ang_dev):
         msg = jnp.where(mine == i, jit_ref[0:1, i : i + 1].astype(jnp.float32), msg)
     jmsg[...] = msg
     jall[me] = msg
     zero = jnp.zeros((SUBS, LANES), jnp.float32)
     for i in range(ang_dev):
-        for t in [0] + list(range(nblocks + 1, ntiles)):
-            fval[i, t] = zero
-            fdif[i, t] = zero
+        for slot in range(fval.shape[0]):
+            for t in [0] + list(range(nblocks + 1, ntiles)):
+                fval[slot, i, t] = zero
+                fdif[slot, i, t] = zero
     for b in range(nblocks):
         acc[b] = zero
 
@@ -192,6 +195,13 @@
         xcopy(k).start()
         ycopy(k).start()
 
+    half = (bins - 1) / 2
+    first_row = (me * rows_dev).astype(jnp.float32) - (nrows - 1) / 2
+    moved = jnp.zeros((SUBS, LANES), jnp.int32)
+    for a in range(angles):
+        moved = jnp.where(lane == a, shift_ref[a], moved)
+    center = half + moved.astype(jnp.float32) + LANES
+
     @pl.loop(1, width)
     def _(i):
         jcopy(i).wait()
@@ -199,25 +209,40 @@
     jit = jall[0]
     for i in range(1, width):
         jit = jit + jall[i]
+    jit = jnp.broadcast_to(jit, (SUBS, LANES))
     ahead = pltpu.roll(jit, LANES - 1, 1)
     behind = pltpu.roll(jit, 1, 1)
     weight = (1.0 + (ahead - behind) * 1.5) * (4.0 / math.sqrt(angles))
     theta = ((lane % angles).astype(jnp.float32) + jit) * math.pi / angles
-    pvec[...] = jnp.where(
-        sub == 0, jnp.cos(theta), jnp.where(sub == 1, jnp.sin(theta), weight)
+    cosine = jnp.cos(theta)
+    sine = jnp.sin(theta)
+    least = jnp.minimum(cosine * (LANES - 1), 0.0) + jnp.minimum(
+        first_row * sine, (first_row + (rows_dev - 1)) * sine
     )
-    move = pltpu.make_async_copy(pvec, psm, lsem.at[1])
-    move.start()
-    move.wait()
-
-    half = (bins - 1) / 2
-    first_row = (me * rows_dev).astype(jnp.float32) - (nrows - 1) / 2
+    for g in range(nblocks // SUBS):
+        group = slice(g * SUBS, (g + 1) * SUBS)
+        start = ((sub + g * SUBS) * LANES).astype(jnp.float32) - half
+        base = start * cosine + center
+        low = (base + least - 0.25).astype(jnp.int32) // LANES
+        low = jnp.minimum(jnp.maximum(low, 0), ntiles - 2)
+        tvec[group] = low
+        pvec[group] = base - (low * LANES).astype(jnp.float32)
+    pvec[nblocks:] = jnp.where(sub == 0, cosine, jnp.where(sub == 1, sine, weight))
+    moves = [
+        pltpu.make_async_copy(pvec, psm, lsem.at[1]),
+        pltpu.make_async_copy(tvec, tsm, lsem.at[2]),
+    ]
+    for move in moves:
+        move.start()
+    for move in moves:
+        move.wait()
+
     rowf = (sub // slices).astype(jnp.float32) + first_row
     low_half = sub < slices
 
-    def project(chunk):
+    def spread(chunk, slot):
         after = [None] * ang_dev
-        wts = [psm[2, chunk * ang_dev + i] for i in range(ang_dev)]
+        wts = [psm[nblocks + 2, chunk * ang_dev + i] for i in range(ang_dev)]
         for t in range(nblocks - 1, -2, -1):
             if t >= 0:
                 h, q, k = t // (nblocks // 2), (t // (nblocks // 4)) % 2, t % (nblocks // 4)
@@ -234,24 +259,18 @@
             for i in range(ang_dev):
                 rolled = pltpu.roll(pair[i], LANES - 1, 1)
                 nxt = zero if after[i] is None else after[i]
-                fdif[i, t + 1] = jnp.where(lane == LANES - 1, nxt, rolled) - pair[i]
+                fdif[slot, i, t + 1] = jnp.where(lane == LANES - 1, nxt, rolled) - pair[i]
                 if t >= 0:
-                    fval[i, t + 1] = pair[i]
+                    fval[slot, i, t + 1] = pair[i]
                 after[i] = rolled
+
+    def add_up(chunk, slot, sums):
         for i in range(ang_dev):
             a = chunk * ang_dev + i
-            cosine = psm[0, a]
-            sine = psm[1, a]
-            center = half + shift_ref[a].astype(jnp.float32)
-            ramp = lanef * cosine + rowf * sine
-            least = jnp.minimum(cosine * (LANES - 1), 0.0) + jnp.minimum(
-                first_row * sine, (first_row + (rows_dev - 1)) * sine
-            )
+            ramp = lanef * psm[nblocks, a] + rowf * psm[nblocks + 1, a]
             for b in range(nblocks):
-                base = (b * LANES - half) * cosine + center + LANES
-                low = (base + least - 0.25).astype(jnp.int32) // LANES
-                low = jnp.minimum(jnp.maximum(low, 0), ntiles - 2)
-                u = ramp + (base - (low * LANES).astype(jnp.float32))
+                low = tsm[b, a]
+                u = ramp + psm[b, a]
                 bin_lo = u.astype(jnp.int32)
                 frac = u - bin_lo.astype(jnp.float32)
                 where = jnp.bitwise_and(bin_lo, LANES - 1)
@@ -260,34 +279,45 @@
                 def pick(ref):
                     return jnp.where(
                         first,
-                        jnp.take_along_axis(ref[i, low], where, axis=1, mode="promise_in_bounds"),
+                        jnp.take_along_axis(ref[slot, i, low], where, axis=1, mode="promise_in_bounds"),
                         jnp.take_along_axis(
-                            ref[i, low + 1], where, axis=1, mode="promise_in_bounds"
+                            ref[slot, i, low + 1], where, axis=1, mode="promise_in_bounds"
                         ),
                     )
 
-                acc[b] += pick(fval) + frac * pick(fdif)
+                got = pick(fval) + frac * pick(fdif)
+                sums[b] = got if sums[b] is None else sums[b] + got
+
+    def project(*group):
+        for slot, chunk in enumerate(group):
+            spread(chunk, slot)
+        sums = [None] * nblocks
+        for slot, chunk in enumerate(group):
+            add_up(chunk, slot, sums)
+        for b in range(nblocks):
+            acc[b] += sums[b]
 
     def corner(k):
         relay_x(k).wait_recv()
         relay_y(k).wait_recv()
+
+    project(me)
+
+    @pl.loop(1, depth)
+    def _(k):
+        relay(k)
+        project(at(me, k), at(xpeer, k - 1), at(ypeer, k - 1))
+
+    corner(0)
+    project(at(xpeer, depth - 1), at(ypeer, depth - 1), at(diag, 0))
+
+    @pl.loop(1, depth - 1)
+    def _(k):
+        corner(k)
         project(at(diag, k))
 
-    project(me)
-
-    @pl.loop(1, depth)
-    def _(k):
-        relay(k)
-        project(at(me, k))
-        project(at(xpeer, k - 1))
-        project(at(ypeer, k - 1))
-
-    project(at(xpeer, depth - 1))
-    project(at(ypeer, depth - 1))
-
-    @pl.loop(0, depth)
-    def _(k):
-        corner(k)
+    corner(depth - 1)
+    project(at(diag, depth - 1))
 
     for b in range(nblocks):
         done = acc[b]
@@ -327,14 +357,16 @@
         scratch_shapes=[
             pltpu.VMEM(slab.shape, jnp.bfloat16),
             pltpu.VMEM((width, 2, 2 * SUBS, bins // 4), jnp.bfloat16),
-            pltpu.VMEM((SUBS, LANES), jnp.float32),
-            pltpu.VMEM((width, SUBS, LANES), jnp.float32),
-            pltpu.VMEM((SUBS, LANES), jnp.float32),
-            pltpu.SMEM((SUBS, LANES), jnp.float32),
-            pltpu.VMEM((ang_dev, ntiles, SUBS, LANES), jnp.float32),
-            pltpu.VMEM((ang_dev, ntiles, SUBS, LANES), jnp.float32),
+            pltpu.VMEM((1, LANES), jnp.float32),
+            pltpu.VMEM((width, 1, LANES), jnp.float32),
+            pltpu.VMEM((bins // LANES + SUBS, LANES), jnp.float32),
+            pltpu.SMEM((bins // LANES + SUBS, LANES), jnp.float32),
+            pltpu.VMEM((bins // LANES, LANES), jnp.int32),
+            pltpu.SMEM((bins // LANES, LANES), jnp.int32),
+            pltpu.VMEM((3, ang_dev, ntiles, SUBS, LANES), jnp.float32),
+            pltpu.VMEM((3, ang_dev, ntiles, SUBS, LANES), jnp.float32),
             pltpu.VMEM((bins // LANES, SUBS, LANES), jnp.float32),
-            dma((2,)),
+            dma((3,)),
             dma((width,)),
             dma((width,)),
             dma((depth,)),

time: 22.4 us -> 21 us (0.938)
  Pallas kernels: 21.6 us -> 20.1 us
    pallas_call x1, Pallas kernels: 21.6 us -> 20.1 us  [body(): pl.pallas_call(functools.partial(kernel, width), out_shape=pltpu.VMEM((ro...]
where the time goes in v3:
time: 21 us; the launch traced here: 20.8 us
  Pallas kernels  20.1 us (96%)
  local copies, waits for them, and re-layouts  0.63 us (3%)
    pallas_call x1, Pallas kernels, body(): pl.pallas_call(functools.partial(kernel, width), out_shape=pltpu.VMEM((ro...  20.1 us
    unnamed x1, local copies, waits for them, and re-layouts  0.63 us

profile of v3, /device:TPU:0, one launch (start us, length us, event | category | flops | bytes accessed | tf_op | source)
XLA Modules:
  0.0 20.8 jit_solution(3811090773419114417)
XLA Ops:
  0.0 20.1 %shard_map.46 = f32[2,4,2048]{2,1,0:T(4,128)S(1)} custom-call(bf16[1,2]{1,0:T(2,128)(2,1)} %bitcast.1, s32[32]{0:T(128)} %shift_ref.1, bf16[2,4,2048]{2,1,0:T(4,128)(2,1)} %sino_ref.1, bf16[256,3840]{1,0:T(8,128)(2,1)} %constant.2.clone.slab_hbm), custom_call_target="tpu_custom_call" | custom-call | tf_op jit(solution)/shard_map/pallas_call | solution.py:352
  20.2 0.6 %copy.6 = f32[2,4,2048]{2,1,0:T(4,128)} copy(f32[2,4,2048]{2,1,0:T(4,128)S(1)} %shard_map.46) | data formatting | bytes 131072
